TPU v7x, 256 devices: a whole 4x4x8 slice. The times are simulated.
256 devices in a mesh: region: 8 (over x, core), sub: 32 (over y, z).
Axes of the slice: x: 4, y: 4, z: 8, core: 2. Of those that a mesh axis runs over, the one named last changes fastest.
Arguments:
- multipliers: float32 [256, 3, 3, 256], P(('region', 'sub')), may hold values from -6 to 6
- direction: float32 [256, 3, 3, 256], P(('region', 'sub')), may hold values from -12 to 12
- residual: float32 [256, 3, 3, 256], P(('region', 'sub')), may hold values from -12 to 12
- reaction: float32 [256, 16, 256], P(('region', 'sub')), may hold values from 0.1 to 2
- viscosity: float32 [256, 16, 256], P(('region', 'sub')), may hold values from 0.5 to 5
- primal_index: int32 [256, 96], P(('region', 'sub')), may hold values from 17 to 2286, as said below
- region_inverse: float32 [8, 3072, 3072], P('region', 'sub'), as said below
- coarse_map: float32 [256, 96, 384], P(('region', 'sub')), may hold values from -0.4375 to 0.4375
- global_inverse: float32 [384, 384], replicated, as said below
Outputs:
- new_multipliers: float32 [256, 3, 3, 256], P(('region', 'sub'))
- new_residual: float32 [256, 3, 3, 256], P(('region', 'sub'))
- velocity: float32 [256, 3, 16, 256], P(('region', 'sub'))
- pressure: float32 [256, 16, 256], P(('region', 'sub'))
Inputs may be any that keep to these rules, and one draw needn't show every extreme that they name: `primal_index`: each row holds 96 different positions, each in the interior of a face (neither face index 0 nor 16 - 1); every row contains the first such position and the last one. `region_inverse`: each region's matrix is symmetric positive definite. `global_inverse`: symmetric positive definite.
All inputs are finite; a program needn't handle non-finite values.
Results may differ from a plain program's by a relative error of at most 0.0001.
Values sent between devices are 32-bit elements; how exact they have to be, the bound alone decides.
A program may use at most 64 MiB of HBM per device.

v0:
```python
import jax
import jax.numpy as jnp
from jax import lax
from jax.sharding import PartitionSpec as P

DOM_Z = 4
LEVELS = 3
SWEEPS = 1
COARSE_SWEEPS = 8
VCYCLES = 2
damping = 0.8


def shifted_2(x, axis, by):
    count = lax.axis_size(axis)
    return lax.ppermute(x, axis, [(i, (i + by) % count) for i in range(count)])


def operate(field, react, weight, cells):
    width = field.shape[-1]
    padded = jnp.pad(field, ((0, 0), (1, 1), (cells, cells)))
    middle = padded[:, 1:-1]
    position = lax.broadcasted_iota(jnp.int32, (1, 1, width), 2) % cells
    above = jnp.where(position < cells - 1, middle[:, :, cells + 1 : cells + 1 + width], 0.0)
    beneath = jnp.where(position > 0, middle[:, :, cells - 1 : cells - 1 + width], 0.0)
    beside = padded[:, 2:, cells : cells + width] + padded[:, :-2, cells : cells + width]
    beside = beside + middle[:, :, 2 * cells :] + middle[:, :, :width]
    beside = beside + above + beneath
    return react * field + weight * (6.0 * field - beside)


def restrict(array, cells):
    lead = array.shape[:-2]
    depth = array.shape[-2]
    half = cells // 2
    blocks = array.reshape(lead + (depth // 2, 2, half, 2, half, 2)).mean(axis=(-5, -3, -1))
    return blocks.reshape(lead + (depth // 2, half * half))


def prolong(array, cells):
    lead = array.shape[:-2]
    depth = array.shape[-2]
    cubic = array.reshape(lead + (depth, cells, cells))
    grown = jnp.repeat(jnp.repeat(jnp.repeat(cubic, 2, axis=-3), 2, axis=-2), 2, axis=-1)
    return grown.reshape(lead + (2 * depth, 4 * cells * cells))


def relax(field, source, react, weight, cells, count):
    diagonal = react + 6.0 * weight
    for _ in range(count):
        field = field + damping * (source - operate(field, react, weight, cells)) / diagonal
    return field


def vcycle(field, source, reacts, cells, level):
    weight = 0.25**level
    if level == LEVELS - 1:
        return relax(field, source, reacts[level], weight, cells, COARSE_SWEEPS)
    field = relax(field, source, reacts[level], weight, cells, SWEEPS)
    remain = restrict(source - operate(field, reacts[level], weight, cells), cells)
    coarse = vcycle(jnp.zeros_like(remain), remain, reacts, cells // 2, level + 1)
    field = field + prolong(coarse, cells // 2)
    return relax(field, source, reacts[level], weight, cells, SWEEPS)


def local_solve(source, react, cells):
    reacts = [react]
    size_now = cells
    for _ in range(LEVELS - 1):
        reacts.append(restrict(reacts[-1], size_now))
        size_now = size_now // 2
    field = jnp.zeros_like(source)
    for _ in range(VCYCLES):
        field = vcycle(field, source, reacts, cells, 0)
    return field


def face_cells(picked, cells):
    face = cells * cells
    block = picked // (3 * face)
    component = picked // face % 3
    spot = picked % face
    first = spot // cells
    second = spot % cells
    upper = cells - 1
    place = jnp.where(
        block == 0,
        upper * face + spot,
        jnp.where(
            block == 1, first * face + upper * cells + second, first * face + second * cells + upper
        ),
    )
    return component * (cells * face) + place


def body(
    multipliers,
    direction,
    residual,
    reaction,
    viscosity,
    primal_index,
    region_inverse,
    coarse_map,
    global_inverse,
):
    highest = lax.Precision.HIGHEST
    react = reaction[0]
    cells = react.shape[0]
    face = react.shape[1]
    upper_end = cells - 1
    active = direction[0]
    below_x = shifted_2(active[0], "region", 1)
    below_y = shifted_2(active[1], "sub", DOM_Z)
    below_z = shifted_2(active[2], "sub", 1)
    source = jnp.zeros((3, cells, face), jnp.float32)
    source = source.at[:, upper_end, :].add(active[0])
    source = source.at[:, :, face - cells :].add(active[1].reshape(3, cells, cells))
    source = source.at[:, :, upper_end::cells].add(active[2].reshape(3, cells, cells))
    source = source.at[:, 0, :].add(-below_x)
    source = source.at[:, :, :cells].add(-below_y.reshape(3, cells, cells))
    source = source.at[:, :, 0::cells].add(-below_z.reshape(3, cells, cells))
    picked = primal_index[0]
    primal = jnp.take(active.reshape(-1), picked)
    rows = region_inverse[0]
    mapping = coarse_map[0]
    share = jnp.dot(primal, mapping, precision=highest)
    total = lax.psum(share, ("region", "sub"))
    region_part = jnp.dot(
        rows, lax.all_gather(primal, "sub", axis=0, tiled=True), precision=highest
    )
    top = jnp.dot(global_inverse, total, precision=highest)
    lifted = region_part + jnp.dot(mapping, top, precision=highest)
    base = local_solve(source, react, cells)
    spots = face_cells(picked, cells)
    velocity = base.reshape(-1).at[spots].add(lifted).reshape(3, cells, face)
    upper_x = velocity[:, upper_end, :]
    upper_y = velocity[:, :, face - cells :].reshape(3, face)
    upper_z = velocity[:, :, upper_end::cells].reshape(3, face)
    lower_x = velocity[:, 0, :]
    lower_y = velocity[:, :, :cells].reshape(3, face)
    lower_z = velocity[:, :, 0::cells].reshape(3, face)
    squares = jnp.sum(residual[0] * residual[0])
    after_x = shifted_2(lower_x, "region", -1)
    after_y = shifted_2(lower_y, "sub", -DOM_Z)
    after_z = shifted_2(lower_z, "sub", -1)
    jump = jnp.stack([upper_x - after_x, upper_y - after_y, upper_z - after_z])
    curvature, squares_all = lax.psum((jnp.sum(active * jump), squares), ("region", "sub"))
    step_x = jnp.concatenate([velocity[0, 1:], after_x[0][None]], axis=0) - velocity[0]
    step_y = (
        jnp.concatenate([velocity[1][:, cells:], after_y[1].reshape(cells, cells)], axis=1)
        - velocity[1]
    )
    position = lax.broadcasted_iota(jnp.int32, (1, face), 1) % cells
    edge_values = jnp.repeat(after_z[2].reshape(cells, cells), cells, axis=1)
    shifted = jnp.pad(velocity[2][:, 1:], ((0, 0), (0, 1)))
    step_z = jnp.where(position == cells - 1, edge_values, shifted) - velocity[2]
    pressure = -viscosity[0] * (step_x + step_y + step_z)
    alpha = squares_all / curvature
    new_multipliers = (multipliers[0] + alpha * active)[None]
    new_residual = (residual[0] - alpha * jump)[None]
    return (new_multipliers, new_residual, velocity[None], pressure[None])


def solution(mesh):
    in_specs = (
        P(("region", "sub"), None, None, None),
        P(("region", "sub"), None, None, None),
        P(("region", "sub"), None, None, None),
        P(("region", "sub"), None, None),
        P(("region", "sub"), None, None),
        P(("region", "sub"), None),
        P("region", "sub", None),
        P(("region", "sub"), None, None),
        P(),
    )
    out_specs = (
        P(("region", "sub"), None, None, None),
        P(("region", "sub"), None, None, None),
        P(("region", "sub"), None, None, None),
        P(("region", "sub"), None, None),
    )
    return jax.shard_map(body, mesh=mesh, in_specs=in_specs, out_specs=out_specs, check_vma=False)
```

profile of v0, /device:TPU:1, one launch (start us, length us, event | category | flops | bytes accessed | tf_op | source)
XLA Modules:
  0.0 369.7 jit_solution(10086883032054162801)
XLA Ops:
  1.5 2.6 collective-permute-start
  4.1 6.9 %collective-permute-start.1 = (f32[3,256]{1,0:T(4,128)S(1)}, f32[3,256]{1,0:T(4,128)S(1)}, u32[]{:S(2)}, u32[]{:S(2)}) collective-permute-start(f32[3,256]{1,0:T(4,128)S(1)} %bitcast.181), channel_id=1, source_target_pairs={{0,4},{1,5},{2,6},{3,7},{4,8},{5,9},{6,10},{7,11},{8,12},{9,13},{1... | collective-permute-start | bytes 9224 | tf_op jit(solution)/shard_map/ppermute | solution.py:16
  13.2 1.7 reshape_squeeze.17
  16.5 1.1 gather_fusion
  19.1 114.8 %all-reduce.28 = f32[3072]{0:T(1024)S(1)} all-reduce(f32[3072]{0:T(1024)S(1)} %fusion.269), channel_id=1, replica_groups=mesh['region'=8,'sub'=32] {'sub'}, use_global_device_ids=true, to_apply=%add.28 | all-reduce | flops 3072 | bytes 24576
  134.0 100.0 %psum.22 = f32[384]{0:T(512)S(1)} all-reduce(f32[384]{0:T(512)S(1)} %convolution_reduce_fusion), channel_id=1, replica_groups=mesh['region'=8,'sub'=32] {'region','sub'}, use_global_device_ids=true, to_apply=%region_10.11 | all-reduce | flops 384 | bytes 3072 | tf_op jit(solution)/shard_map/psum | solution.py:128
  239.4 4.3 %scatter-add.44 = f32[3,16,256]{1,0,2:T(4,128)S(1)} dynamic-update-slice(f32[3,16,256]{1,0,2:T(4,128)S(1)} %scatter_fusion, f32[3,1,256]{1,0,2:T(4,128)S(1)} %slice_add_fusion, s32[]{:T(128)} %constant.334.clone.1, s32[]{:T(128)} %constant.334.clone.1, s32[]{:T(128)} %constant.334.clone.1) | dynamic-update-slice | bytes 6148 | tf_op jit(solution)/shard_map/scatter-add | solution.py:120
  244.8 2.0 fusion.17
  246.9 2.0 add_subtract_fusion.1
  249.0 4.8 %reshape.713 = f32[3,8,2,8,2,8,2]{6,5,4,3,2,1,0:T(8,128)} reshape(f32[3,16,256]{2,1,0:T(8,128)S(1)} %copy.135) | data formatting | bytes 98304 | tf_op jit(solution)/shard_map/reshape | solution.py:36
  253.8 2.2 reduce_sum.73
  259.1 2.1 bitcast_add_fusion.1
  261.2 2.1 divide_add_fusion.2
  263.3 2.1 divide_add_fusion.1
  265.3 2.2 add_subtract_fusion
  267.7 4.8 %reshape.721 = f32[3,8,2,8,2,8,2]{6,5,4,3,2,1,0:T(8,128)} reshape(f32[3,16,256]{2,1,0:T(8,128)S(1)} %copy.147) | data formatting | bytes 98304 | tf_op jit(solution)/shard_map/reshape | solution.py:36
  272.5 2.2 reduce_sum.77
  277.9 2.1 divide_add_fusion
  280.2 1.1 scatter_fusion.2
  281.4 1.1 collective-permute-start.3
  283.6 1.3 collective-permute-start.5
  285.0 2.1 collective-permute-start.4
  287.8 3.6 collective-permute-done.4
  292.1 74.3 %all-reduce.29 = (f32[]{:T(128)}, f32[]{:T(128)}) all-reduce(f32[]{:T(128)} %multiply_reduce_fusion, f32[]{:T(128)} %fusion.100), channel_id=1, replica_groups=mesh['region'=8,'sub'=32] {'region','sub'}, use_global_device_ids=true, to_apply=%region_1.0 | all-reduce | flops 2 | bytes 16 | tf_op jit(solution)/shard_map/psum | solution.py:148
  (186 shorter events, 22.8 us)
Async XLA Ops:
  0.6 234.1 %copy-start = (f32[1,96,3072]{2,1,0:T(8,128)S(1)}, f32[1,96,3072]{2,1,0:T(8,128)}, u32[]{:S(2)}) copy-start(f32[1,96,3072]{2,1,0:T(8,128)} %param.23) | copy-start | bytes 3538948
  1.5 237.1 %collective-permute-start = (f32[3,256]{1,0:T(4,128)S(1)}, f32[3,256]{1,0:T(4,128)S(1)}, u32[]{:S(2)}, u32[]{:S(2)}) collective-permute-start(f32[3,256]{1,0:T(4,128)S(1)} %bitcast.182), channel_id=1, source_target_pairs={{0,32},{32,64},{64,96},{96,128},{128,160},{160,192},{192,224},{224... | collective-permute-start | bytes 9224 | tf_op jit(solution)/shard_map/ppermute | solution.py:16
  4.1 234.8 %collective-permute-start.1 = (f32[3,256]{1,0:T(4,128)S(1)}, f32[3,256]{1,0:T(4,128)S(1)}, u32[]{:S(2)}, u32[]{:S(2)}) collective-permute-start(f32[3,256]{1,0:T(4,128)S(1)} %bitcast.181), channel_id=1, source_target_pairs={{0,4},{1,5},{2,6},{3,7},{4,8},{5,9},{6,10},{7,11},{8,12},{9,13},{1... | collective-permute-start | bytes 9224 | tf_op jit(solution)/shard_map/ppermute | solution.py:16
  11.0 228.0 %collective-permute-start.2 = (f32[3,256]{1,0:T(4,128)S(1)}, f32[3,256]{1,0:T(4,128)S(1)}, u32[]{:S(2)}, u32[]{:S(2)}) collective-permute-start(f32[3,256]{1,0:T(4,128)S(1)} %bitcast.180), channel_id=1, source_target_pairs={{0,1},{1,2},{2,3},{3,4},{4,5},{5,6},{6,7},{7,8},{8,9},{9,10},{10,1... | collective-permute-start | bytes 9224 | tf_op jit(solution)/shard_map/ppermute | solution.py:16
  15.1 1.3 copy-start.8
  15.1 1.3 copy-start.4
  15.4 2.3 copy-start.9
  15.4 118.4 %copy-start.2 = (f32[1,96,384]{2,1,0:T(8,128)S(1)}, f32[1,96,384]{2,1,0:T(8,128)}, u32[]{:S(2)}) copy-start(f32[1,96,384]{2,1,0:T(8,128)} %param.24) | copy-start | bytes 442372
  15.6 218.4 %copy-start.5 = (f32[1,3,3,256]{3,0,2,1:T(1,128)S(1)}, f32[1,3,3,256]{3,0,2,1:T(1,128)}, u32[]{:S(2)}) copy-start(f32[1,3,3,256]{3,0,2,1:T(1,128)} %param.19) | copy-start | bytes 27652
  16.0 219.7 %copy-start.1 = (f32[384,384]{1,0:T(8,128)S(1)}, f32[384,384]{1,0:T(8,128)}, u32[]{:S(2)}) copy-start(f32[384,384]{1,0:T(8,128)} %param.25) | copy-start | bytes 1769476
  234.7 2.4 copy-start.3
  280.2 88.2 %copy-start.7 = (f32[1,3,3,256]{3,0,2,1:T(1,128)S(1)}, f32[1,3,3,256]{3,0,2,1:T(1,128)}, u32[]{:S(2)}) copy-start(f32[1,3,3,256]{3,0,2,1:T(1,128)} %param.17) | copy-start | bytes 27652
  280.2 88.8 %copy-start.6 = (f32[1,16,256]{2,1,0:T(8,128)S(1)}, f32[1,16,256]{2,1,0:T(8,128)}, u32[]{:S(2)}) copy-start(f32[1,16,256]{2,1,0:T(8,128)} %param.21) | copy-start | bytes 49156
  281.4 6.0 %collective-permute-start.3 = (f32[3,256]{1,0:T(4,128)S(1)}, f32[3,256]{1,0:T(4,128)S(1)}, u32[]{:S(2)}, u32[]{:S(2)}) collective-permute-start(f32[3,256]{1,0:T(4,128)S(1)} %bitcast.183), channel_id=1, source_target_pairs={{0,224},{32,0},{64,32},{96,64},{128,96},{160,128},{192,160},{224,1... | collective-permute-start | bytes 9224 | tf_op jit(solution)/shard_map/ppermute | solution.py:16
  283.6 3.8 %collective-permute-start.5 = (f32[3,256]{1,0:T(4,128)S(1)}, f32[3,256]{1,0:T(4,128)S(1)}, u32[]{:S(2)}, u32[]{:S(2)}) collective-permute-start(f32[3,256]{1,0:T(4,128)S(1)} %reshape.734), channel_id=1, source_target_pairs={{0,31},{1,0},{2,1},{3,2},{4,3},{5,4},{6,5},{7,6},{8,7},{9,8},{10,9... | collective-permute-start | bytes 9224 | tf_op jit(solution)/shard_map/ppermute | solution.py:16
  285.0 6.4 %collective-permute-start.4 = (f32[3,256]{1,0:T(4,128)S(1)}, f32[3,256]{1,0:T(4,128)S(1)}, u32[]{:S(2)}, u32[]{:S(2)}) collective-permute-start(f32[3,256]{1,0:T(4,128)S(1)} %reshape.732), channel_id=1, source_target_pairs={{0,28},{1,29},{2,30},{3,31},{4,0},{5,1},{6,2},{7,3},{8,4},{9,5},{1... | collective-permute-start | bytes 9224 | tf_op jit(solution)/shard_map/ppermute | solution.py:16
where the time goes:
time: 371 us; the launch traced here: 370 us
  blocking collectives  289 us (78%)
  other arithmetic  29.4 us (8%)
  local copies, waits for them, and re-layouts  27.2 us (7%)
  starting transfers between devices  14.8 us (4%)
    unnamed x1, blocking collectives  115 us
    psum x1, blocking collectives, body(): total = lax.psum(share, ('region', 'sub'))  100 us
    psum x1, blocking collectives, body(): lax.psum((jnp.sum(active * jump), squares), ('region', 'sub'))  74.3 us
    ppermute x6, starting transfers between devices, shifted_2(): return lax.ppermute(x, axis, [(i, (i + by) % count) for i in range(count)])  14.8 us
    reshape x4, local copies, waits for them, and re-layouts, restrict(): array.reshape(lead + (depth // 2, 2, half, 2, half, 2))  10.7 us
    add x17, other arithmetic, relax(): field + damping * (source - operate(field, react, weight, cells)) / diagonal  7.44 us
  transfers between devices with their start and end apart: 6, of which 1 were waited for; matrix products, arithmetic and copies ran while one was open for 4% of the time, Pallas kernels for 0%

commit v1 on v0

--- a/solution.py
+++ b/solution.py
@@ -125,7 +125,7 @@
     rows = region_inverse[0]
     mapping = coarse_map[0]
     share = jnp.dot(primal, mapping, precision=highest)
-    total = lax.psum(share, ("region", "sub"))
+    total = lax.psum(lax.psum(share, "region"), "sub")
     region_part = jnp.dot(
         rows, lax.all_gather(primal, "sub", axis=0, tiled=True), precision=highest
     )

time: 371 us -> 308 us (0.83)
  blocking collectives: 289 us -> 198 us
  starting transfers between devices: 14.8 us -> 41.3 us
    psum x1, blocking collectives: 100 us -> 11.3 us  [body(): total = lax.psum(lax.psum(share, 'region'), 'sub')]
    ppermute x6, starting transfers between devices: 14.8 us -> 41.3 us  [shifted_2(): return lax.ppermute(x, axis, [(i, (i + by) % count) for i in range(count)])]
  transfers between devices with their start and end apart: 6 -> 6, of which waited for: 1 -> 2; matrix products, arithmetic and copies ran while one was open for 4% -> 4% of each run, Pallas kernels for 0% -> 0%
where the time goes in v1:
time: 308 us; the launch traced here: 307 us
  blocking collectives  198 us (64%)
  starting transfers between devices  41.3 us (13%)
  other arithmetic  29.4 us (10%)
  local copies, waits for them, and re-layouts  27.2 us (9%)
  waiting for transfers between devices  5.68 us (2%)
  between operations  3.48 us (1%)
    unnamed x1, blocking collectives  114 us
    psum x1, blocking collectives, body(): lax.psum((jnp.sum(active * jump), squares), ('region', 'sub'))  72.8 us
    ppermute x6, starting transfers between devices, shifted_2(): return lax.ppermute(x, axis, [(i, (i + by) % count) for i in range(count)])  41.3 us
    psum x1, blocking collectives, body(): total = lax.psum(lax.psum(share, 'region'), 'sub')  11.3 us
    reshape x4, local copies, waits for them, and re-layouts, restrict(): array.reshape(lead + (depth // 2, 2, half, 2, half, 2))  10.7 us
    add x17, other arithmetic, relax(): field + damping * (source - operate(field, react, weight, cells)) / diagonal  7.44 us
  transfers between devices with their start and end apart: 6, of which 2 were waited for; matrix products, arithmetic and copies ran while one was open for 4% of the time, Pallas kernels for 0%

profile of v1, /device:TPU:1, one launch (start us, length us, event | category | flops | bytes accessed | tf_op | source)
XLA Modules:
  0.0 307.4 jit_solution(1538200924350504840)
XLA Ops:
  1.5 2.6 collective-permute-start
  4.1 6.9 %collective-permute-start.1 = (f32[3,256]{1,0:T(4,128)S(1)}, f32[3,256]{1,0:T(4,128)S(1)}, u32[]{:S(2)}, u32[]{:S(2)}) collective-permute-start(f32[3,256]{1,0:T(4,128)S(1)} %bitcast.181), channel_id=1, source_target_pairs={{0,4},{1,5},{2,6},{3,7},{4,8},{5,9},{6,10},{7,11},{8,12},{9,13},{1... | collective-permute-start | bytes 9224 | tf_op jit(solution)/shard_map/ppermute | solution.py:16
  13.2 1.7 reshape_squeeze.17
  16.5 1.1 gather_fusion
  17.9 11.3 %psum.29 = f32[384]{0:T(512)S(1)} all-reduce(f32[384]{0:T(512)S(1)} %convolution_reduce_fusion), channel_id=1, replica_groups=mesh['region'=8,'sub'=32] {'region'}, use_global_device_ids=true, to_apply=%region_10.11 | all-reduce | flops 384 | bytes 3072 | tf_op jit(solution)/shard_map/psum | solution.py:128
  30.6 114.1 %all-reduce.30 = (f32[3072]{0:T(1024)S(1)}, f32[384]{0:T(512)S(1)}) all-reduce(f32[3072]{0:T(1024)S(1)} %fusion.269, f32[384]{0:T(512)S(1)} %psum.29), channel_id=1, replica_groups=mesh['region'=8,'sub'=32] {'sub'}, use_global_device_ids=true, to_apply=%add.28 | all-reduce | flops 3456 | bytes 27648
  148.1 1.1 scatter_fusion
  150.0 4.3 %scatter-add.44 = f32[3,16,256]{1,0,2:T(4,128)S(1)} dynamic-update-slice(f32[3,16,256]{1,0,2:T(4,128)S(1)} %scatter_fusion, f32[3,1,256]{1,0,2:T(4,128)S(1)} %slice_add_fusion, s32[]{:T(128)} %constant.334.clone.1, s32[]{:T(128)} %constant.334.clone.1, s32[]{:T(128)} %constant.334.clone.1) | dynamic-update-slice | bytes 6148 | tf_op jit(solution)/shard_map/scatter-add | solution.py:120
  155.4 2.0 fusion.17
  157.5 2.0 add_subtract_fusion.1
  159.6 4.8 %reshape.713 = f32[3,8,2,8,2,8,2]{6,5,4,3,2,1,0:T(8,128)} reshape(f32[3,16,256]{2,1,0:T(8,128)S(1)} %copy.135) | data formatting | bytes 98304 | tf_op jit(solution)/shard_map/reshape | solution.py:36
  164.5 2.2 reduce_sum.73
  169.7 2.1 bitcast_add_fusion.1
  171.8 2.1 divide_add_fusion.2
  173.9 2.1 divide_add_fusion.1
  175.9 2.2 add_subtract_fusion
  178.3 4.8 %reshape.721 = f32[3,8,2,8,2,8,2]{6,5,4,3,2,1,0:T(8,128)} reshape(f32[3,16,256]{2,1,0:T(8,128)S(1)} %copy.147) | data formatting | bytes 98304 | tf_op jit(solution)/shard_map/reshape | solution.py:36
  183.1 2.2 reduce_sum.77
  188.5 2.1 divide_add_fusion
  190.8 1.1 scatter_fusion.2
  192.0 31.0 %collective-permute-start.3 = (f32[3,256]{1,0:T(4,128)S(1)}, f32[3,256]{1,0:T(4,128)S(1)}, u32[]{:S(2)}, u32[]{:S(2)}) collective-permute-start(f32[3,256]{1,0:T(4,128)S(1)} %bitcast.183), channel_id=1, source_target_pairs={{0,224},{32,0},{64,32},{96,64},{128,96},{160,128},{192,160},{224,1... | collective-permute-start | bytes 9224 | tf_op jit(solution)/shard_map/ppermute | solution.py:16
  224.7 2.0 collective-permute-done.5
  226.9 3.7 %collective-permute-done.4 = f32[3,256]{1,0:T(4,128)S(1)} collective-permute-done((f32[3,256]{1,0:T(4,128)S(1)}, f32[3,256]{1,0:T(4,128)S(1)}, u32[]{:S(2)}, u32[]{:S(2)}) %collective-permute-start.4) | collective-permute-done | bytes 3104 | tf_op jit(solution)/shard_map/ppermute | solution.py:16
  231.4 72.8 %all-reduce.29 = (f32[]{:T(128)}, f32[]{:T(128)}) all-reduce(f32[]{:T(128)} %multiply_reduce_fusion, f32[]{:T(128)} %fusion.100), channel_id=1, replica_groups=mesh['region'=8,'sub'=32] {'region','sub'}, use_global_device_ids=true, to_apply=%region_1.0 | all-reduce | flops 2 | bytes 16 | tf_op jit(solution)/shard_map/psum | solution.py:148
  (186 shorter events, 21.7 us)
Async XLA Ops:
  0.6 145.3 %copy-start = (f32[1,96,3072]{2,1,0:T(8,128)S(1)}, f32[1,96,3072]{2,1,0:T(8,128)}, u32[]{:S(2)}) copy-start(f32[1,96,3072]{2,1,0:T(8,128)} %param.23) | copy-start | bytes 3538948
  1.5 147.7 %collective-permute-start = (f32[3,256]{1,0:T(4,128)S(1)}, f32[3,256]{1,0:T(4,128)S(1)}, u32[]{:S(2)}, u32[]{:S(2)}) collective-permute-start(f32[3,256]{1,0:T(4,128)S(1)} %bitcast.182), channel_id=1, source_target_pairs={{0,32},{32,64},{64,96},{96,128},{128,160},{160,192},{192,224},{224... | collective-permute-start | bytes 9224 | tf_op jit(solution)/shard_map/ppermute | solution.py:16
  4.1 145.4 %collective-permute-start.1 = (f32[3,256]{1,0:T(4,128)S(1)}, f32[3,256]{1,0:T(4,128)S(1)}, u32[]{:S(2)}, u32[]{:S(2)}) collective-permute-start(f32[3,256]{1,0:T(4,128)S(1)} %bitcast.181), channel_id=1, source_target_pairs={{0,4},{1,5},{2,6},{3,7},{4,8},{5,9},{6,10},{7,11},{8,12},{9,13},{1... | collective-permute-start | bytes 9224 | tf_op jit(solution)/shard_map/ppermute | solution.py:16
  11.0 138.6 %collective-permute-start.2 = (f32[3,256]{1,0:T(4,128)S(1)}, f32[3,256]{1,0:T(4,128)S(1)}, u32[]{:S(2)}, u32[]{:S(2)}) collective-permute-start(f32[3,256]{1,0:T(4,128)S(1)} %bitcast.180), channel_id=1, source_target_pairs={{0,1},{1,2},{2,3},{3,4},{4,5},{5,6},{6,7},{7,8},{8,9},{9,10},{10,1... | collective-permute-start | bytes 9224 | tf_op jit(solution)/shard_map/ppermute | solution.py:16
  15.1 1.3 copy-start.8
  15.1 1.3 copy-start.4
  15.4 2.3 copy-start.2
  15.4 13.9 %copy-start.9 = (u32[256]{0:T(256)S(1)}, u32[256]{0:T(256)}, u32[]{:S(2)}) copy-start(u32[256]{0:T(256)} %constant.426) | copy-start | bytes 3076
  15.6 129.0 %copy-start.5 = (f32[1,3,3,256]{3,0,2,1:T(1,128)S(1)}, f32[1,3,3,256]{3,0,2,1:T(1,128)}, u32[]{:S(2)}) copy-start(f32[1,3,3,256]{3,0,2,1:T(1,128)} %param.19) | copy-start | bytes 27652
  15.7 129.6 %copy-start.1 = (f32[384,384]{1,0:T(8,128)S(1)}, f32[384,384]{1,0:T(8,128)}, u32[]{:S(2)}) copy-start(f32[384,384]{1,0:T(8,128)} %param.25) | copy-start | bytes 1769476
  145.3 2.4 copy-start.3
  190.8 115.3 %copy-start.7 = (f32[1,3,3,256]{3,0,2,1:T(1,128)S(1)}, f32[1,3,3,256]{3,0,2,1:T(1,128)}, u32[]{:S(2)}) copy-start(f32[1,3,3,256]{3,0,2,1:T(1,128)} %param.17) | copy-start | bytes 27652
  190.8 115.9 %copy-start.6 = (f32[1,16,256]{2,1,0:T(8,128)S(1)}, f32[1,16,256]{2,1,0:T(8,128)}, u32[]{:S(2)}) copy-start(f32[1,16,256]{2,1,0:T(8,128)} %param.21) | copy-start | bytes 49156
  192.0 32.6 %collective-permute-start.3 = (f32[3,256]{1,0:T(4,128)S(1)}, f32[3,256]{1,0:T(4,128)S(1)}, u32[]{:S(2)}, u32[]{:S(2)}) collective-permute-start(f32[3,256]{1,0:T(4,128)S(1)} %bitcast.183), channel_id=1, source_target_pairs={{0,224},{32,0},{64,32},{96,64},{128,96},{160,128},{192,160},{224,1... | collective-permute-start | bytes 9224 | tf_op jit(solution)/shard_map/ppermute | solution.py:16
  224.1 2.5 collective-permute-start.5
  224.3 6.4 %collective-permute-start.4 = (f32[3,256]{1,0:T(4,128)S(1)}, f32[3,256]{1,0:T(4,128)S(1)}, u32[]{:S(2)}, u32[]{:S(2)}) collective-permute-start(f32[3,256]{1,0:T(4,128)S(1)} %reshape.732), channel_id=1, source_target_pairs={{0,28},{1,29},{2,30},{3,31},{4,0},{5,1},{6,2},{7,3},{8,4},{9,5},{1... | collective-permute-start | bytes 9224 | tf_op jit(solution)/shard_map/ppermute | solution.py:16
